TPU v7x, 512 devices: a whole 4x8x8 slice. The times are simulated.
512 devices in a mesh: section: 16 (over x, z_hi), tensor: 32 (over y, z_lo, core).
Axes of the slice: x: 4, y: 8, z: 8 (z_hi: 4, z_lo: 2; z = z_hi * 2 + z_lo), core: 2. Of those that a mesh axis runs over, the one named last changes fastest.
Arguments:
- x_in: bfloat16 [16, 512, 4096], P('section', 'tensor'), may hold values from -40 to 40
- grad_out: bfloat16 [16, 512, 4096], P('section', 'tensor'), may hold values from -50 to 50
- gain: float32 [16, 4096], P('section'), may hold values from 0.5 to 1.5
- w_val: bfloat16 [16, 4096, 4096], P('section', 'tensor'), may hold values from -0.09375 to 0.09375
- w_out: bfloat16 [16, 4096, 4096], P('section', 'tensor'), may hold values from -0.09375 to 0.09375
- filt: float32 [16, 3, 4096], P('section', None, 'tensor'), may hold values from -3 to 3
- tail: bfloat16 [16, 2, 4096], P('section', None, 'tensor'), may hold values from -6 to 6
- micro_index: int32 [16], P('section'), may hold values from 0 to 15
Outputs:
- grad_in: bfloat16 [16, 512, 4096], P('section', 'tensor')
- grad_w_val: bfloat16 [16, 4096, 4096], P('section', 'tensor')
- grad_w_out: bfloat16 [16, 4096, 4096], P('section', 'tensor')
- grad_filter: float32 [16, 3, 4096], P('section', None, 'tensor')
- grad_tail: float32 [16, 2, 4096], P('section', None, 'tensor')
- grad_gain: float32 [16, 4096], P('section')
All inputs are finite; a program needn't handle non-finite values.
Results may differ from a plain program's by a relative error of at most 0.023.
Values may be sent and summed in bfloat16 or wider, within the bound.
No kernel may reach another device: no remote copies, remote signals or barrier semaphores. Data moves between devices by JAX's collectives and lax.ppermute only.
A program may use at most 64 MiB of HBM per device.

v0:
```python
import jax
import jax.numpy as jnp
from jax import lax
from jax.sharding import PartitionSpec as P

TAPS = 3
EPSILON = 1e-06


def shifted(block, axis, distance):
    devices = range(lax.axis_size(axis))
    route = [((i - distance) % len(devices), i) for i in devices]
    return lax.ppermute(block, axis, route)


def contract_last(left, right):
    return lax.dot_general(
        left, right, (((1,), (1,)), ((), ())), preferred_element_type=jnp.float32
    )


def contract_first(left, right):
    return lax.dot_general(
        left, right, (((0,), (0,)), ((), ())), preferred_element_type=jnp.float32
    )


def on_device(x_in, grad_out, gain, w_val, w_out, filt, tail, micro_index):
    x_rows = x_in[0]
    cot_rows = grad_out[0]
    gain_row = gain[0]
    val_weight = w_val[0]
    out_weight = w_out[0]
    filters = filt[0]
    tail_rows = tail[0]
    has_tail = micro_index[0] > 0
    x_float = x_rows.astype(jnp.float32)
    inv_rms = lax.rsqrt(jnp.mean(x_float * x_float, axis=-1, keepdims=True) + EPSILON)
    normed = (x_float * inv_rms * gain_row).astype(jnp.bfloat16)
    normed_all = lax.all_gather(normed, "tensor", axis=0, tiled=True)
    seq_len = normed_all.shape[0]
    values = contract_last(normed_all, val_weight).astype(jnp.bfloat16)
    lead_rows = jnp.where(has_tail, tail_rows, jnp.zeros_like(tail_rows))
    extended = jnp.concatenate([lead_rows, values], axis=0).astype(jnp.float32)
    conv_out = filters[0] * extended[TAPS - 1 : TAPS - 1 + seq_len]
    for tap in range(1, TAPS):
        conv_out = conv_out + filters[tap] * extended[TAPS - 1 - tap : TAPS - 1 - tap + seq_len]
    gate_sig = jax.nn.sigmoid(conv_out)
    gated = (conv_out * gate_sig).astype(jnp.bfloat16)
    grad_gated = contract_last(lax.all_gather(cot_rows, "tensor", axis=0, tiled=True), out_weight)
    grad_wo = contract_first(gated, lax.all_gather(cot_rows, "tensor", axis=0, tiled=True))
    grad_conv = grad_gated * gate_sig * (1.0 + conv_out * (1.0 - gate_sig))
    grad_filter = jnp.stack(
        [
            jnp.sum(grad_conv * extended[TAPS - 1 - tap : TAPS - 1 - tap + seq_len], axis=0)
            for tap in range(TAPS)
        ]
    )
    padded = jnp.pad(grad_conv, ((TAPS - 1, TAPS - 1), (0, 0)))
    grad_ext = filters[0] * padded[0 : seq_len + TAPS - 1]
    for tap in range(1, TAPS):
        grad_ext = grad_ext + filters[tap] * padded[tap : tap + seq_len + TAPS - 1]
    grad_values = grad_ext[TAPS - 1 :].astype(jnp.bfloat16)
    grad_tail = jnp.where(has_tail, grad_ext[: TAPS - 1], jnp.zeros_like(grad_ext[: TAPS - 1]))
    grad_wv = contract_first(grad_values, normed_all)
    grad_normed = lax.psum_scatter(
        jnp.dot(grad_values, val_weight, preferred_element_type=jnp.float32).astype(jnp.bfloat16),
        "tensor",
        scatter_dimension=0,
        tiled=True,
    ).astype(jnp.float32)
    gain_term = jnp.sum(grad_normed * x_float * inv_rms, axis=0)
    grad_gain = lax.psum(gain_term, "tensor")
    scaled = gain_row * grad_normed
    grad_local = (
        cot_rows.astype(jnp.float32)
        + inv_rms * scaled
        - x_float * inv_rms**3 * jnp.mean(scaled * x_float, axis=-1, keepdims=True)
    )
    received = shifted(grad_local.astype(jnp.bfloat16), "section", -1)
    return (
        received[None],
        grad_wv.astype(jnp.bfloat16)[None],
        grad_wo.astype(jnp.bfloat16)[None],
        grad_filter[None],
        grad_tail[None],
        grad_gain[None],
    )


def solution(mesh):
    placed = (
        P("section", "tensor", None),
        P("section", "tensor", None),
        P("section", None),
        P("section", "tensor", None),
        P("section", "tensor", None),
        P("section", None, "tensor"),
        P("section", None, "tensor"),
        P("section"),
    )
    return jax.shard_map(
        on_device,
        mesh=mesh,
        in_specs=placed,
        out_specs=(
            P("section", "tensor", None),
            P("section", "tensor", None),
            P("section", "tensor", None),
            P("section", None, "tensor"),
            P("section", None, "tensor"),
            P("section", None),
        ),
        check_vma=False,
    )
```

profile of v0, /device:TPU:32, one launch (start us, length us, event | category | flops | bytes accessed | tf_op | source)
XLA Modules:
  0.0 413.5 jit_solution(13749967059140600081)
XLA Ops:
  7.2 0.0 copy-start
  7.2 0.0 copy-start.5
  7.2 0.0 all-gather.4.cloned.1.call-start
  7.2 1.2 fusion.18
  8.4 1.7 fusion.20
  10.1 0.0 all-gather.4.cloned.1.call-update
  10.1 0.0 all-gather.6.cloned.1.call-start
  10.2 0.7 all-gather.6.cloned.1.call-update
  10.9 0.0 reduce-scatter.2.cloned.1.call-start
  11.6 0.7 fusion.27
  12.2 0.7 slice_bitcast_fusion.2
  12.9 69.8 %all-gather.4.cloned.1.call-done = bf16[512,4096]{1,0:T(8,128)(2,1)} async-done(((bf16[16,4096]{1,0:T(8,128)(2,1)}), bf16[512,4096]{1,0:T(8,128)(2,1)}) %all-gather.4.cloned.1.call-update) | async-done | bytes 4194320 | tf_op jit(solution)/shard_map/all_gather | solution.py:40
  82.7 0.0 copy-done
  82.7 3.4 convolution_convert_fusion.3
  86.2 0.1 multiply_add_fusion.1
  86.3 67.6 %all-gather.6.cloned.1.call-done = bf16[1,512,4096]{2,1,0:T(8,128)(2,1)} async-done(((bf16[1,16,4096]{2,1,0:T(8,128)(2,1)}), bf16[1,512,4096]{2,1,0:T(8,128)(2,1)}) %all-gather.6.cloned.1.call-update) | async-done | bytes 4194320 | tf_op jit(solution)/shard_map/all_gather | solution.py:50
  153.9 0.0 copy-done.5
  153.9 3.5 multiply_reduce_fusion.2
  157.4 0.1 multiply_add_fusion
  157.5 3.2 convolution_convert_fusion
  160.7 0.0 reduce-scatter.2.cloned.1.call-update
  160.8 0.0 copy-start.1
  160.8 0.6 copy.14
  161.3 0.0 copy-start.2
  161.3 0.0 copy-start.4
  161.4 4.2 %fusion.1 = bf16[1,128,4096]{2,1,0:T(8,128)(2,1)} fusion(bf16[1,512,4096]{2,1,0:T(8,128)(2,1)} %all-gather.6.cloned.1.call-done, f32[512,128]{1,0:T(8,128)S(1)} %multiply_add_fusion.1), kind=kOutput, calls=%fused_computation.4 | convolution fusion | flops 537722880 | bytes 5505024 | tf_op jit(solution)/shard_map/dot_general | solution.py:23
  165.6 0.0 copy-done.1
  165.6 0.0 copy-start.3
  165.6 1.7 fusion
  167.3 120.2 %reduce-scatter.2.cloned.1.call-done = bf16[16,4096]{1,0:T(8,128)(2,1)} async-done(((bf16[512,4096]{1,0:T(8,128)(2,1)}), bf16[16,4096]{1,0:T(8,128)(2,1)}) %reduce-scatter.2.cloned.1.call-update) | async-done | bytes 131088 | tf_op jit(solution)/shard_map/reduce_scatter | solution.py:66
  287.6 0.0 copy-done.2
  287.6 0.0 copy-done.4
  287.6 1.2 fusion.24
  288.7 0.0 copy-done.3
  288.7 1.0 fusion.17
  289.8 7.5 %collective-permute-start = (bf16[16,4096]{1,0:T(8,128)(2,1)S(1)}, bf16[16,4096]{1,0:T(8,128)(2,1)S(1)}, u32[]{:S(2)}, u32[]{:S(2)}) collective-permute-start(bf16[16,4096]{1,0:T(8,128)(2,1)S(1)} %fusion.17), channel_id=1, source_target_pairs={{32,0},{64,32},{96,64},{128,96},{160,128},{192,160},{224,192},{256... | collective-permute-start | bytes 393224 | tf_op jit(solution)/shard_map/ppermute | solution.py:13
  297.3 0.6 fusion.26
  297.9 108.5 %psum.7 = f32[1,4096]{1,0:T(1,128)} all-reduce(f32[1,4096]{1,0:T(1,128)S(1)} %bitcast.60), channel_id=1, replica_groups=mesh['section'=16,'tensor'=32] {'tensor'}, use_global_device_ids=true, to_apply=%region_7.8 | all-reduce | flops 4096 | bytes 32768 | tf_op jit(solution)/shard_map/psum | solution.py:73
  406.3 0.0 collective-permute-done
  406.3 0.7 copy.17
  (4 shorter events, 0.1 us)
Async XLA Ops:
  7.2 75.6 %copy-start = (bf16[1,128,4096]{2,1,0:T(8,128)(2,1)S(1)}, bf16[1,128,4096]{2,1,0:T(8,128)(2,1)}, u32[]{:S(2)}) copy-start(bf16[1,128,4096]{2,1,0:T(8,128)(2,1)} %param.11) | copy-start | bytes 3145732
  7.2 146.8 %copy-start.5 = (bf16[1,128,4096]{2,1,0:T(8,128)(2,1)S(1)}, bf16[1,128,4096]{2,1,0:T(8,128)(2,1)}, u32[]{:S(2)}) copy-start(bf16[1,128,4096]{2,1,0:T(8,128)(2,1)} %param.12) | copy-start | bytes 3145732
  7.2 75.5 %all-gather.4.cloned.1.call-start = ((), (), s32[]{:S(2)}) async-start(), calls=%async_computation.1 | async-start | bytes 4325376 | tf_op jit(solution)/shard_map/all_gather | solution.py:40
  10.1 143.8 %all-gather.6.cloned.1.call-start = ((), (), s32[]{:S(2)}) async-start(), calls=%async_computation.3 | async-start | bytes 4325376 | tf_op jit(solution)/shard_map/all_gather | solution.py:50
  10.9 276.7 %reduce-scatter.2.cloned.1.call-start = ((), (), s32[]{:S(2)}) async-start(), calls=%async_computation.2 | async-start | bytes 4325376 | tf_op jit(solution)/shard_map/reduce_scatter | solution.py:66
  160.8 4.8 %copy-start.1 = (bf16[512,4096]{1,0:T(8,128)(2,1)S(1)}, bf16[512,4096]{1,0:T(8,128)(2,1)}, u32[]{:S(2)}) copy-start(bf16[512,4096]{1,0:T(8,128)(2,1)} %all-gather.4.cloned.1.call-done) | copy-start | bytes 12582916
  161.3 126.2 %copy-start.2 = (bf16[1,16,4096]{2,1,0:T(8,128)(2,1)S(1)}, bf16[1,16,4096]{2,1,0:T(8,128)(2,1)}, u32[]{:S(2)}) copy-start(bf16[1,16,4096]{2,1,0:T(8,128)(2,1)} %param.8) | copy-start | bytes 393220
  161.3 126.2 %copy-start.4 = (f32[1,4096]{1,0:T(1,128)S(1)}, f32[1,4096]{1,0:T(1,128)}, u32[]{:S(2)}) copy-start(f32[1,4096]{1,0:T(1,128)} %param.10) | copy-start | bytes 49156
  165.6 123.1 %copy-start.3 = (bf16[1,16,4096]{2,1,0:T(8,128)(2,1)S(1)}, bf16[1,16,4096]{2,1,0:T(8,128)(2,1)}, u32[]{:S(2)}) copy-start(bf16[1,16,4096]{2,1,0:T(8,128)(2,1)} %param.9) | copy-start | bytes 393220
  289.8 116.6 %collective-permute-start = (bf16[16,4096]{1,0:T(8,128)(2,1)S(1)}, bf16[16,4096]{1,0:T(8,128)(2,1)S(1)}, u32[]{:S(2)}, u32[]{:S(2)}) collective-permute-start(bf16[16,4096]{1,0:T(8,128)(2,1)S(1)} %fusion.17), channel_id=1, source_target_pairs={{32,0},{64,32},{96,64},{128,96},{160,128},{192,160},{224,192},{256... | collective-permute-start | bytes 393224 | tf_op jit(solution)/shard_map/ppermute | solution.py:13
Sparse Core Ops, SparseCore 0:
  10.7 71.9 all-gather.3
  84.9 69.0 all-gather.5
  160.9 126.6 reduce-scatter.1
where the time goes:
time: 414 us
  waiting for transfers between devices  258 us (62%)
  blocking collectives  108 us (26%)
  matrix products  16.1 us (4%)
  between operations  14.5 us (4%)
  starting transfers between devices  7.63 us (2%)
  other arithmetic  6.52 us (2%)
    reduce_scatter x1, waiting for transfers between devices, on_device(): lax.psum_scatter(jnp.dot(grad_values, val_weight, preferred_element_type=...  120 us
    psum x1, blocking collectives, on_device(): grad_gain = lax.psum(gain_term, 'tensor')  108 us
    all_gather x1, waiting for transfers between devices, on_device(): normed_all = lax.all_gather(normed, 'tensor', axis=0, tiled=True)  69.8 us
    all_gather x1, waiting for transfers between devices, on_device(): lax.all_gather(cot_rows, 'tensor', axis=0, tiled=True)  67.6 us
  transfers between devices with their start and end apart: 4, of which 3 were waited for; matrix products, arithmetic and copies ran while one was open for 3% of the time, Pallas kernels for 0%

commit v1 on v0

--- a/solution.py
+++ b/solution.py
@@ -70,7 +70,7 @@
         tiled=True,
     ).astype(jnp.float32)
     gain_term = jnp.sum(grad_normed * x_float * inv_rms, axis=0)
-    grad_gain = lax.psum(gain_term, "tensor")
+    grad_gain = jnp.sum(lax.all_gather(gain_term, "tensor"), axis=0)
     scaled = gain_row * grad_normed
     grad_local = (
         cot_rows.astype(jnp.float32)

time: 414 us -> 341 us (0.82)
  the two profiles are of different devices: /device:TPU:32 before, /device:TPU:1 now
where the time goes in v1:
time: 341 us
  waiting for transfers between devices  258 us (76%)
  blocking collectives  35.4 us (10%)
  matrix products  15.9 us (5%)
  between operations  14.5 us (4%)
  starting transfers between devices  7.58 us (2%)
  other arithmetic  7.17 us (2%)
    reduce_scatter x1, waiting for transfers between devices, on_device(): lax.psum_scatter(jnp.dot(grad_values, val_weight, preferred_element_type=...  117 us
    all_gather x1, waiting for transfers between devices, on_device(): normed_all = lax.all_gather(normed, 'tensor', axis=0, tiled=True)  73.1 us
    all_gather x1, waiting for transfers between devices, on_device(): lax.all_gather(cot_rows, 'tensor', axis=0, tiled=True)  67.6 us
    all_gather x1, blocking collectives, on_device(): grad_gain = jnp.sum(lax.all_gather(gain_term, 'tensor'), axis=0)  35.4 us
    ppermute x1, starting transfers between devices, shifted(): return lax.ppermute(block, axis, route)  7.46 us
    dot_general x2, matrix products, contract_last(): lax.dot_general(left, right, (((1,), (1,)), ((), ())), preferred_element_...  6.91 us
  transfers between devices with their start and end apart: 4, of which 3 were waited for; matrix products, arithmetic and copies ran while one was open for 4% of the time, Pallas kernels for 0%

profile of v1, /device:TPU:1, one launch (start us, length us, event | category | flops | bytes accessed | tf_op | source)
XLA Modules:
  0.0 341.0 jit_solution(7701724642571612917)
XLA Ops:
  7.2 0.0 copy-start
  7.2 0.0 copy-start.5
  7.2 0.0 all-gather.5.cloned.1.call-start
  7.2 1.2 fusion.18
  8.4 1.7 fusion.20
  10.1 0.0 all-gather.5.cloned.1.call-update
  10.1 0.0 all-gather.7.cloned.1.call-start
  10.2 0.7 all-gather.7.cloned.1.call-update
  10.9 0.0 reduce-scatter.2.cloned.1.call-start
  11.6 0.7 fusion.27
  12.2 0.7 slice_bitcast_fusion.2
  12.9 73.1 %all-gather.5.cloned.1.call-done = bf16[512,4096]{1,0:T(8,128)(2,1)} async-done(((bf16[16,4096]{1,0:T(8,128)(2,1)}), bf16[512,4096]{1,0:T(8,128)(2,1)}) %all-gather.5.cloned.1.call-update) | async-done | bytes 4194320 | tf_op jit(solution)/shard_map/all_gather | solution.py:40
  86.0 0.0 copy-done
  86.0 3.4 %convolution_convert_fusion.3 = bf16[512,128]{1,0:T(8,128)(2,1)S(1)} fusion(bf16[512,4096]{1,0:T(8,128)(2,1)} %all-gather.5.cloned.1.call-done, bf16[1,128,4096]{2,1,0:T(8,128)(2,1)S(1)} %copy-done), kind=kOutput, calls=%fused_computation.10 | convolution fusion | flops 536936448 | bytes 5373952 | tf_op jit(solution)/shard_map/dot_general | solution.py:17
  89.5 0.1 multiply_add_fusion.1
  89.6 67.6 %all-gather.7.cloned.1.call-done = bf16[1,512,4096]{2,1,0:T(8,128)(2,1)} async-done(((bf16[1,16,4096]{2,1,0:T(8,128)(2,1)}), bf16[1,512,4096]{2,1,0:T(8,128)(2,1)}) %all-gather.7.cloned.1.call-update) | async-done | bytes 4194320 | tf_op jit(solution)/shard_map/all_gather | solution.py:50
  157.2 0.0 copy-done.5
  157.2 3.5 %multiply_reduce_fusion.2 = (f32[128]{0:T(128)S(1)}, f32[128]{0:T(128)S(1)}, f32[128]{0:T(128)S(1)}, f32[512,128]{1,0:T(8,128)S(1)}) fusion(f32[514,128]{1,0:T(8,128)S(1)} %maximum_convert_fusion, f32[512,128]{1,0:T(8,128)S(1)} %multiply_add_fusion.1, bf16[1,128,4096]{2,1,0:T(8,128)(2,1)S(1)} %copy-done.5, ...), kind=kOutput, calls=%fused_computation.35 | convolution fusion | flops 537788032 | bytes 6555136 | tf_op jit(solution)/shard_map/dot_general | solution.py:17
  160.7 0.1 multiply_add_fusion
  160.8 3.2 convolution_convert_fusion
  164.0 0.0 reduce-scatter.2.cloned.1.call-update
  164.0 0.0 copy-start.1
  164.1 0.6 copy.16
  164.6 0.6 fusion.26
  165.2 0.0 copy-start.2
  165.2 0.0 copy-start.4
  165.2 4.0 %fusion.1 = bf16[1,128,4096]{2,1,0:T(8,128)(2,1)} fusion(bf16[1,512,4096]{2,1,0:T(8,128)(2,1)} %all-gather.7.cloned.1.call-done, f32[512,128]{1,0:T(8,128)S(1)} %multiply_add_fusion.1), kind=kOutput, calls=%fused_computation.4 | convolution fusion | flops 537722880 | bytes 5505024 | tf_op jit(solution)/shard_map/dot_general | solution.py:23
  169.2 0.0 copy-done.1
  169.2 0.0 copy-start.3
  169.2 1.7 fusion
  171.0 117.0 %reduce-scatter.2.cloned.1.call-done = bf16[16,4096]{1,0:T(8,128)(2,1)} async-done(((bf16[512,4096]{1,0:T(8,128)(2,1)}), bf16[16,4096]{1,0:T(8,128)(2,1)}) %reduce-scatter.2.cloned.1.call-update) | async-done | bytes 131088 | tf_op jit(solution)/shard_map/reduce_scatter | solution.py:66
  288.0 0.0 copy-done.2
  288.0 0.0 copy-done.4
  288.0 1.2 fusion.24
  289.1 0.0 copy-done.3
  289.1 1.0 fusion.17
  290.2 7.5 %collective-permute-start = (bf16[16,4096]{1,0:T(8,128)(2,1)S(1)}, bf16[16,4096]{1,0:T(8,128)(2,1)S(1)}, u32[]{:S(2)}, u32[]{:S(2)}) collective-permute-start(bf16[16,4096]{1,0:T(8,128)(2,1)S(1)} %fusion.17), channel_id=1, source_target_pairs={{32,0},{64,32},{96,64},{128,96},{160,128},{192,160},{224,192},{256... | collective-permute-start | bytes 393224 | tf_op jit(solution)/shard_map/ppermute | solution.py:13
  297.6 35.4 %all-gather.1 = f32[131072]{0:T(1024)S(1)} all-gather(f32[4096]{0:T(1024)S(1)} %get-tuple-element.27), channel_id=3, replica_groups=mesh['section'=16,'tensor'=32] {'tensor'}, dimensions={0}, use_global_device_ids=true | all-gather | bytes 540672 | tf_op jit(solution)/shard_map/all_gather | solution.py:73
  333.0 0.1 reshape.45
  333.1 0.7 reduce_sum.69
  333.8 0.0 collective-permute-done
  333.8 0.7 copy.19
  (4 shorter events, 0.1 us)
Async XLA Ops:
  7.2 78.9 %copy-start = (bf16[1,128,4096]{2,1,0:T(8,128)(2,1)S(1)}, bf16[1,128,4096]{2,1,0:T(8,128)(2,1)}, u32[]{:S(2)}) copy-start(bf16[1,128,4096]{2,1,0:T(8,128)(2,1)} %param.11) | copy-start | bytes 3145732
  7.2 150.1 %copy-start.5 = (bf16[1,128,4096]{2,1,0:T(8,128)(2,1)S(1)}, bf16[1,128,4096]{2,1,0:T(8,128)(2,1)}, u32[]{:S(2)}) copy-start(bf16[1,128,4096]{2,1,0:T(8,128)(2,1)} %param.12) | copy-start | bytes 3145732
  7.2 78.8 %all-gather.5.cloned.1.call-start = ((), (), s32[]{:S(2)}) async-start(), calls=%async_computation.1 | async-start | bytes 4325376 | tf_op jit(solution)/shard_map/all_gather | solution.py:40
  10.1 147.1 %all-gather.7.cloned.1.call-start = ((), (), s32[]{:S(2)}) async-start(), calls=%async_computation.3 | async-start | bytes 4325376 | tf_op jit(solution)/shard_map/all_gather | solution.py:50
  10.9 277.1 %reduce-scatter.2.cloned.1.call-start = ((), (), s32[]{:S(2)}) async-start(), calls=%async_computation.2 | async-start | bytes 4325376 | tf_op jit(solution)/shard_map/reduce_scatter | solution.py:66
  164.0 5.2 %copy-start.1 = (bf16[512,4096]{1,0:T(8,128)(2,1)S(1)}, bf16[512,4096]{1,0:T(8,128)(2,1)}, u32[]{:S(2)}) copy-start(bf16[512,4096]{1,0:T(8,128)(2,1)} %all-gather.5.cloned.1.call-done) | copy-start | bytes 12582916
  165.2 122.8 %copy-start.2 = (bf16[1,16,4096]{2,1,0:T(8,128)(2,1)S(1)}, bf16[1,16,4096]{2,1,0:T(8,128)(2,1)}, u32[]{:S(2)}) copy-start(bf16[1,16,4096]{2,1,0:T(8,128)(2,1)} %param.8) | copy-start | bytes 393220
  165.2 122.8 %copy-start.4 = (f32[1,4096]{1,0:T(1,128)S(1)}, f32[1,4096]{1,0:T(1,128)}, u32[]{:S(2)}) copy-start(f32[1,4096]{1,0:T(1,128)} %param.10) | copy-start | bytes 49156
  169.2 119.9 %copy-start.3 = (bf16[1,16,4096]{2,1,0:T(8,128)(2,1)S(1)}, bf16[1,16,4096]{2,1,0:T(8,128)(2,1)}, u32[]{:S(2)}) copy-start(bf16[1,16,4096]{2,1,0:T(8,128)(2,1)} %param.9) | copy-start | bytes 393220
  290.2 43.6 %collective-permute-start = (bf16[16,4096]{1,0:T(8,128)(2,1)S(1)}, bf16[16,4096]{1,0:T(8,128)(2,1)S(1)}, u32[]{:S(2)}, u32[]{:S(2)}) collective-permute-start(bf16[16,4096]{1,0:T(8,128)(2,1)S(1)} %fusion.17), channel_id=1, source_target_pairs={{32,0},{64,32},{96,64},{128,96},{160,128},{192,160},{224,192},{256... | collective-permute-start | bytes 393224 | tf_op jit(solution)/shard_map/ppermute | solution.py:13
Sparse Core Ops, SparseCore 0:
  10.7 75.2 all-gather.4
  88.2 69.0 all-gather.6
  164.2 123.7 reduce-scatter.1
